TPU v7x, 32 devices: a whole 2x2x4 slice. The times are simulated.
32 devices in a mesh: rows: 8 (over y, x, core), feat: 4 (over z).
Axes of the slice: x: 2, y: 2, z: 4, core: 2. Of those that a mesh axis runs over, the one named last changes fastest.
Arguments:
- features: bfloat16 [1536, 16384], P('rows', 'feat'), may hold values from -0.5 to 0.5
- labels: int32 [1536], P('rows'), may hold values 0 or 1
- posterior: bfloat16 [16384], P('feat'), may hold values from -1 to 1
- prior_prec: float32 [16384], P('feat'), may hold values from 1 to 10
Outputs:
- hessian: float32 [16384, 16384], P('feat', 'rows')
- gradient: float32 [16384], P('feat')
All inputs are finite; a program needn't handle non-finite values. No bound on the sum of `labels` on one device may be relied on, other than what follows from the above.
Results may differ from a plain program's by a relative error of at most 0.003.
Values may be sent and summed in bfloat16 or wider, within the bound.
A program may use at most 128 MiB of HBM per device.

v0:
```python
import jax
import jax.numpy as jnp
from jax import lax
from jax.sharding import PartitionSpec as P


def per_device(features, labels, posterior, prior_prec):
    row_count = lax.axis_size("rows")
    feat_count = lax.axis_size("feat")
    row_index = lax.axis_index("rows")
    feat_index = lax.axis_index("feat")
    block_width = features.shape[1]
    col_width = block_width * feat_count // row_count
    partial_value = jnp.dot(features, posterior, preferred_element_type=jnp.float32)
    margins = lax.psum(partial_value, "feat")
    chance = jax.nn.sigmoid(margins)
    weight = (chance * (1.0 - chance)).astype(jnp.bfloat16)
    residual = (labels.astype(jnp.float32) - chance).astype(jnp.bfloat16)
    all_rows, all_weight = (
        lax.all_gather(features, "rows", axis=0, tiled=True),
        lax.all_gather(weight, "rows", axis=0, tiled=True),
    )
    local_grad = jnp.dot(residual, features, preferred_element_type=jnp.float32)
    summed = lax.psum(local_grad, "rows")
    gradient = summed - prior_prec * posterior.astype(jnp.float32)
    full_width = lax.all_gather(features, "feat", axis=1, tiled=True)
    column_rows = lax.all_to_all(full_width, "rows", split_axis=1, concat_axis=0, tiled=True)
    weighted = all_weight[:, None] * all_rows
    product = lax.dot_general(
        weighted, column_rows, (((0,), (0,)), ((), ())), preferred_element_type=jnp.float32
    )
    global_rows = feat_index * block_width + jnp.arange(block_width, dtype=jnp.int32)
    global_cols = row_index * col_width + jnp.arange(col_width, dtype=jnp.int32)
    on_diagonal = global_rows[:, None] == global_cols[None, :]
    hessian = product + jnp.where(on_diagonal, prior_prec[:, None], jnp.float32(0.0))
    return (hessian, gradient)


def solution(mesh):
    in_specs = (P("rows", "feat"), P("rows"), P("feat"), P("feat"))
    out_specs = (P("feat", "rows"), P("feat"))
    return jax.shard_map(
        per_device, mesh=mesh, in_specs=in_specs, out_specs=out_specs, check_vma=False
    )
```

profile of v0, /device:TPU:0, one launch (start us, length us, event | category | flops | bytes accessed | tf_op | source)
XLA Modules:
  0.0 306.3 jit_solution(11984968131884465313)
XLA Ops:
  7.2 0.0 all-gather.5.cloned.1.call-start
  7.2 0.7 all-gather.5.cloned.1.call-update
  7.9 0.0 all-gather.3.cloned.1.call-start
  7.9 0.7 all-gather.3.cloned.1.call-update
  8.6 119.0 %all-gather.5.cloned.1.call-done = bf16[192,16384]{1,0:T(8,128)(2,1)} async-done(((bf16[192,4096]{1,0:T(8,128)(2,1)}), bf16[192,16384]{1,0:T(8,128)(2,1)}) %all-gather.5.cloned.1.call-update) | async-done | bytes 6291472 | tf_op jit(solution)/shard_map/all_gather | solution.py:26
  127.6 0.0 copy-start.1
  127.6 0.0 copy-start
  127.6 0.0 copy-start.3
  127.6 0.0 copy-start.4
  127.6 0.0 copy-start.2
  127.6 6.7 %copy.10 = bf16[24,8,8,2048]{3,2,0,1:T(8,128)(2,1)} copy(bf16[24,8,8,2048]{3,2,1,0:T(8,128)(2,1)} %bitcast.16) | data formatting | bytes 12582912 | tf_op jit(solution)/shard_map/all_to_all | solution.py:27
  134.4 4.9 %all-to-all-start = ((bf16[192,8,2048]{2,0,1:T(8,128)(2,1)}), bf16[192,8,2048]{2,0,1:T(8,128)(2,1)}, u32[]{:S(2)}, u32[]{:S(2)}) async-start(bf16[192,8,2048]{2,0,1:T(8,128)(2,1)} %bitcast.15), calls=%async_computation | async-start | bytes 12582912 | tf_op jit(solution)/shard_map/all_to_all | solution.py:27
  139.3 0.0 copy-done.1
  139.3 0.0 copy-done
  139.3 0.5 fusion.3
  139.8 8.6 %psum.14 = f32[192]{0:T(256)S(1)} all-reduce(f32[192]{0:T(256)S(1)} %bitcast.18), channel_id=1, replica_groups=mesh['rows'=8,'feat'=4] {'feat'}, use_global_device_ids=true, to_apply=%region_0.0 | all-reduce | flops 192 | bytes 1536 | tf_op jit(solution)/shard_map/psum | solution.py:15
  148.4 0.0 copy-done.3
  148.4 0.0 copy-done.4
  148.4 0.6 dynamic-slice
  149.7 0.2 dynamic-update-slice
  149.9 90.2 %all-reduce = bf16[1536]{0:T(1024)(128)(2,1)S(1)} all-reduce(bf16[1536]{0:T(1024)(128)(2,1)S(1)} %dynamic-update-slice), channel_id=1, replica_groups=mesh['rows'=8,'feat'=4] {'rows'}, use_global_device_ids=true, to_apply=%add | all-reduce | flops 1536 | bytes 6144
  240.1 0.3 fusion.4
  240.4 23.5 %psum.15 = f32[4096]{0:T(1024)S(1)} all-reduce(f32[4096]{0:T(1024)S(1)} %bitcast.17), channel_id=1, replica_groups=mesh['rows'=8,'feat'=4] {'rows'}, use_global_device_ids=true, to_apply=%region_1.0 | all-reduce | flops 4096 | bytes 32768 | tf_op jit(solution)/shard_map/psum | solution.py:24
  263.9 0.0 copy-done.2
  264.0 0.6 multiply_subtract_fusion
  264.6 0.0 all-to-all-done
  264.6 0.0 all-gather.3.cloned.1.call-done
  264.6 34.9 %select_add_fusion = f32[4096,2048]{1,0:T(8,128)} fusion(bf16[1536,2048]{1,0:T(8,128)(2,1)} %bitcast.3, f32[4096]{0:T(1024)S(1)} %copy-done.2, s32[2048]{0:T(1024)S(1)} %iota_add_fusion.1, s32[4096]{0:T(1024)S(1)} %iota_add_fusion, bf16[1536,4096]{1,0:T(8,128)(2,1)} %all-gather.3.cloned.1.call-done, bf16[1536]{0:T(1024)(128)(2,1)S(1)} %all-reduce), kind=kOutput, calls=%fused_computation | convolution fusion | flops 25801261056 | bytes 52472832 | tf_op jit(solution)/shard_map/dot_general | solution.py:29
  (7 shorter events, 0.0 us)
Async XLA Ops:
  7.2 120.5 %all-gather.5.cloned.1.call-start = ((), (), s32[]{:S(2)}) async-start(), calls=%async_computation.2 | async-start | bytes 7864320 | tf_op jit(solution)/shard_map/all_gather | solution.py:26
  7.9 256.7 %all-gather.3.cloned.1.call-start = ((), (), s32[]{:S(2)}) async-start(), calls=%async_computation.1 | async-start | bytes 14155776 | tf_op jit(solution)/shard_map/all_gather | solution.py:20
  127.6 11.6 %copy-start.1 = (bf16[4096]{0:T(1024)(128)(2,1)S(1)}, bf16[4096]{0:T(1024)(128)(2,1)}, u32[]{:S(2)}) copy-start(bf16[4096]{0:T(1024)(128)(2,1)} %param.6) | copy-start | bytes 24580
  127.6 11.7 %copy-start = (bf16[192,4096]{1,0:T(8,128)(2,1)S(1)}, bf16[192,4096]{1,0:T(8,128)(2,1)}, u32[]{:S(2)}) copy-start(bf16[192,4096]{1,0:T(8,128)(2,1)} %param.4) | copy-start | bytes 4718596
  127.6 20.7 %copy-start.3 = (s32[192]{0:T(256)S(1)}, s32[192]{0:T(256)}, u32[]{:S(2)}) copy-start(s32[192]{0:T(256)} %param.5) | copy-start | bytes 2308
  127.6 20.8 %copy-start.4 = (u32[32]{0:T(128)S(1)}, u32[32]{0:T(128)}, u32[]{:S(2)}) copy-start(u32[32]{0:T(128)} %constant.19) | copy-start | bytes 388
  127.6 136.3 %copy-start.2 = (f32[4096]{0:T(1024)S(1)}, f32[4096]{0:T(1024)}, u32[]{:S(2)}) copy-start(f32[4096]{0:T(1024)} %param.7) | copy-start | bytes 49156
  134.4 130.2 %all-to-all-start = ((bf16[192,8,2048]{2,0,1:T(8,128)(2,1)}), bf16[192,8,2048]{2,0,1:T(8,128)(2,1)}, u32[]{:S(2)}, u32[]{:S(2)}) async-start(bf16[192,8,2048]{2,0,1:T(8,128)(2,1)} %bitcast.15), calls=%async_computation | async-start | bytes 12582912 | tf_op jit(solution)/shard_map/all_to_all | solution.py:27
Sparse Core Ops, SparseCore 0:
  9.5 118.0 all-gather.4
  129.5 130.8 all-gather.2
where the time goes:
time: 307 us; the launch traced here: 306 us
  blocking collectives  122 us (40%)
  waiting for transfers between devices  120 us (39%)
  matrix products  35.7 us (12%)
  between operations  14.8 us (5%)
  local copies, waits for them, and re-layouts  7.61 us (2%)
  starting transfers between devices  4.94 us (2%)
    all_gather x1, waiting for transfers between devices, per_device(): full_width = lax.all_gather(features, 'feat', axis=1, tiled=True)  119 us
    unnamed x1, blocking collectives  90.2 us
    dot_general x1, matrix products, per_device(): lax.dot_general(weighted, column_rows, (((0,), (0,)), ((), ())), preferre...  34.9 us
    psum x1, blocking collectives, per_device(): summed = lax.psum(local_grad, 'rows')  23.5 us
    psum x1, blocking collectives, per_device(): margins = lax.psum(partial_value, 'feat')  8.57 us
    all_to_all x1, local copies, waits for them, and re-layouts, per_device(): lax.all_to_all(full_width, 'rows', split_axis=1, concat_axis=0, tiled=True)  6.73 us
  transfers between devices with their start and end apart: 3, of which 1 were waited for; matrix products, arithmetic and copies ran while one was open for 3% of the time, Pallas kernels for 0%

commit v1 on v0

--- a/solution.py
+++ b/solution.py
@@ -2,6 +2,16 @@
 import jax.numpy as jnp
 from jax import lax
 from jax.sharding import PartitionSpec as P
+
+
+def around_the_ring(x, name, dim):
+    count = lax.axis_size(name)
+    moving, shards = (x, [x])
+    for _ in range(count - 1):
+        moving = lax.ppermute(moving, name, [(i, (i + 1) % count) for i in range(count)])
+        shards.insert(0, moving)
+    line = jnp.concatenate(shards, axis=dim)
+    return jnp.roll(line, (lax.axis_index(name) + 1) * x.shape[dim], axis=dim)
 
 
 def per_device(features, labels, posterior, prior_prec):
@@ -23,7 +33,7 @@
     local_grad = jnp.dot(residual, features, preferred_element_type=jnp.float32)
     summed = lax.psum(local_grad, "rows")
     gradient = summed - prior_prec * posterior.astype(jnp.float32)
-    full_width = lax.all_gather(features, "feat", axis=1, tiled=True)
+    full_width = around_the_ring(features, "feat", 1)
     column_rows = lax.all_to_all(full_width, "rows", split_axis=1, concat_axis=0, tiled=True)
     weighted = all_weight[:, None] * all_rows
     product = lax.dot_general(

time: 307 us -> 294 us (0.958)
  blocking collectives: 122 us -> 98.2 us
  local copies, waits for them, and re-layouts: 7.61 us -> 24.7 us
  waiting for transfers between devices: 120 us -> 112 us
    all_gather x1 -> x0, waiting for transfers between devices: 119 us -> none  [per_device(): full_width = lax.all_gather(features, 'feat', axis=1, tiled=True)]
    ppermute x0 -> x3, waiting for transfers between devices: none -> 111 us  [around_the_ring(): lax.ppermute(moving, name, [(i, (i + 1) % count) for i in range(count)])]
    unnamed x1, blocking collectives: 90.2 us -> 67.5 us
    unnamed x14 -> x21, local copies, waits for them, and re-layouts: 0.87 us -> 16.9 us
    all_to_all x1, local copies, waits for them, and re-layouts: 6.73 us -> 3.28 us  [per_device(): lax.all_to_all(full_width, 'rows', split_axis=1, concat_axis=0, tiled=True)]
    dynamic_slice x0 -> x1, local copies, waits for them, and re-layouts: none -> 3.2 us  [around_the_ring(): return jnp.roll(line, (lax.axis_index(name) + 1) * x.shape[dim], axis=dim)]
    ppermute x0 -> x3, starting transfers between devices: none -> 3.11 us  [around_the_ring(): lax.ppermute(moving, name, [(i, (i + 1) % count) for i in range(count)])]
  transfers between devices with their start and end apart: 3 -> 5, of which waited for: 1 -> 3; matrix products, arithmetic and copies ran while one was open for 3% -> 9% of each run, Pallas kernels for 0% -> 0%
where the time goes in v1:
time: 294 us; the launch traced here: 293 us
  waiting for transfers between devices  112 us (38%)
  blocking collectives  98.2 us (33%)
  matrix products  35.6 us (12%)
  local copies, waits for them, and re-layouts  24.7 us (8%)
  between operations  14.8 us (5%)
  starting transfers between devices  7.95 us (3%)
    ppermute x3, waiting for transfers between devices, around_the_ring(): lax.ppermute(moving, name, [(i, (i + 1) % count) for i in range(count)])  111 us
    unnamed x1, blocking collectives  67.5 us
    dot_general x1, matrix products, per_device(): lax.dot_general(weighted, column_rows, (((0,), (0,)), ((), ())), preferre...  34.8 us
    psum x1, blocking collectives, per_device(): summed = lax.psum(local_grad, 'rows')  22.3 us
    unnamed x21, local copies, waits for them, and re-layouts  16.9 us
    psum x1, blocking collectives, per_device(): margins = lax.psum(partial_value, 'feat')  8.35 us
  transfers between devices with their start and end apart: 5, of which 3 were waited for; matrix products, arithmetic and copies ran while one was open for 9% of the time, Pallas kernels for 0%

profile of v1, /device:TPU:0, one launch (start us, length us, event | category | flops | bytes accessed | tf_op | source)
XLA Modules:
  0.0 293.4 jit_solution(17414135304795943936)
XLA Ops:
  7.2 0.0 copy-start
  7.2 0.0 all-gather.2.cloned.1.call-start
  7.2 0.7 all-gather.2.cloned.1.call-update
  7.9 3.1 %collective-permute-start = (bf16[192,4096]{1,0:T(8,128)(2,1)}, bf16[192,4096]{1,0:T(8,128)(2,1)S(1)}, u32[]{:S(2)}, u32[]{:S(2)}) collective-permute-start(bf16[192,4096]{1,0:T(8,128)(2,1)} %param.4), channel_id=1, source_target_pairs={{0,1},{1,2},{2,3},{3,0},{4,5},{5,6},{6,7},{7,4},{8,9},{9,10},{10,1... | collective-permute-start | bytes 4718600 | tf_op jit(solution)/shard_map/ppermute | solution.py:11
  11.0 36.6 %collective-permute-done = bf16[192,4096]{1,0:T(8,128)(2,1)S(1)} collective-permute-done((bf16[192,4096]{1,0:T(8,128)(2,1)}, bf16[192,4096]{1,0:T(8,128)(2,1)S(1)}, u32[]{:S(2)}, u32[]{:S(2)}) %collective-permute-start) | collective-permute-done | bytes 1572896 | tf_op jit(solution)/shard_map/ppermute | solution.py:11
  47.6 0.0 collective-permute-start.1
  47.6 37.5 %collective-permute-done.1 = bf16[192,4096]{1,0:T(8,128)(2,1)} collective-permute-done((bf16[192,4096]{1,0:T(8,128)(2,1)S(1)}, bf16[192,4096]{1,0:T(8,128)(2,1)}, u32[]{:S(2)}, u32[]{:S(2)}) %collective-permute-start.1) | collective-permute-done | bytes 1572896 | tf_op jit(solution)/shard_map/ppermute | solution.py:11
  85.1 36.8 %collective-permute-done.2 = bf16[192,4096]{1,0:T(8,128)(2,1)} collective-permute-done((bf16[192,4096]{1,0:T(8,128)(2,1)}, bf16[192,4096]{1,0:T(8,128)(2,1)}, u32[]{:S(2)}, u32[]{:S(2)}) %collective-permute-start.2) | collective-permute-done | bytes 1572896 | tf_op jit(solution)/shard_map/ppermute | solution.py:11
  121.9 2.7 constant_dynamic-update-slice_fusion.7
  124.6 2.7 constant_dynamic-update-slice_fusion.6
  127.3 1.2 constant_dynamic-update-slice_fusion.5
  128.6 2.7 constant_dynamic-update-slice_fusion.4
  131.3 2.7 constant_dynamic-update-slice_fusion.3
  134.0 2.7 constant_dynamic-update-slice_fusion.2
  136.7 1.2 constant_dynamic-update-slice_fusion.1
  137.9 1.3 constant_dynamic-update-slice_fusion
  139.2 3.2 %constant_dynamic-slice_fusion = bf16[192,16384]{1,0:T(8,128)(2,1)S(1)} fusion(bf16[192,32768]{1,0:T(8,128)(2,1)} %constant_dynamic-update-slice_fusion, s32[]{:T(128)S(6)} %select_n.18), kind=kLoop, calls=%fused_computation.19 | loop fusion | bytes 12582916 | tf_op jit(solution)/shard_map/jit(_roll_dynamic)/dynamic_slice | solution.py:14
  142.4 0.0 copy-start.1
  142.5 0.0 copy-start.3
  142.5 0.0 copy-start.4
  142.5 0.0 copy-start.2
  142.5 3.3 %copy.10 = bf16[24,8,8,2048]{3,2,0,1:T(8,128)(2,1)} copy(bf16[24,8,8,2048]{3,2,1,0:T(8,128)(2,1)S(1)} %bitcast.16) | data formatting | bytes 12582912 | tf_op jit(solution)/shard_map/all_to_all | solution.py:37
  145.8 4.8 %all-to-all-start = ((bf16[192,8,2048]{2,0,1:T(8,128)(2,1)}), bf16[192,8,2048]{2,0,1:T(8,128)(2,1)}, u32[]{:S(2)}, u32[]{:S(2)}) async-start(bf16[192,8,2048]{2,0,1:T(8,128)(2,1)} %bitcast.15), calls=%async_computation | async-start | bytes 12582912 | tf_op jit(solution)/shard_map/all_to_all | solution.py:37
  150.6 0.5 fusion.3
  151.1 8.4 %psum.14 = f32[192]{0:T(256)S(1)} all-reduce(f32[192]{0:T(256)S(1)} %bitcast.18), channel_id=1, replica_groups=mesh['rows'=8,'feat'=4] {'feat'}, use_global_device_ids=true, to_apply=%region_0.0 | all-reduce | flops 192 | bytes 1536 | tf_op jit(solution)/shard_map/psum | solution.py:25
  159.5 0.6 dynamic-slice
  160.8 0.2 dynamic-update-slice
  161.0 67.5 %all-reduce = bf16[1536]{0:T(1024)(128)(2,1)S(1)} all-reduce(bf16[1536]{0:T(1024)(128)(2,1)S(1)} %dynamic-update-slice), channel_id=1, replica_groups=mesh['rows'=8,'feat'=4] {'rows'}, use_global_device_ids=true, to_apply=%add | all-reduce | flops 1536 | bytes 6144
  228.5 0.3 fusion.4
  228.8 22.3 %psum.15 = f32[4096]{0:T(1024)S(1)} all-reduce(f32[4096]{0:T(1024)S(1)} %bitcast.17), channel_id=1, replica_groups=mesh['rows'=8,'feat'=4] {'rows'}, use_global_device_ids=true, to_apply=%region_1.0 | all-reduce | flops 4096 | bytes 32768 | tf_op jit(solution)/shard_map/psum | solution.py:34
  251.2 0.6 multiply_subtract_fusion
  251.8 34.8 %select_add_fusion = f32[4096,2048]{1,0:T(8,128)} fusion(bf16[1536,2048]{1,0:T(8,128)(2,1)} %bitcast.3, f32[4096]{0:T(1024)S(1)} %copy-done.2, s32[2048]{0:T(1024)S(1)} %iota_add_fusion.1, s32[4096]{0:T(1024)S(1)} %iota_add_fusion, bf16[1536,4096]{1,0:T(8,128)(2,1)} %all-gather.2.cloned.1.call-done, bf16[1536]{0:T(1024)(128)(2,1)S(1)} %all-reduce), kind=kOutput, calls=%fused_computation | convolution fusion | flops 25801261056 | bytes 52472832 | tf_op jit(solution)/shard_map/dot_general | solution.py:39
  (15 shorter events, 0.1 us)
Async XLA Ops:
  7.2 130.8 %copy-start = (bf16[192,4096]{1,0:T(8,128)(2,1)S(1)}, bf16[192,4096]{1,0:T(8,128)(2,1)}, u32[]{:S(2)}) copy-start(bf16[192,4096]{1,0:T(8,128)(2,1)} %param.4) | copy-start | bytes 4718596
  7.2 244.6 %all-gather.2.cloned.1.call-start = ((), (), s32[]{:S(2)}) async-start(), calls=%async_computation.1 | async-start | bytes 14155776 | tf_op jit(solution)/shard_map/all_gather | solution.py:30
  7.9 39.7 %collective-permute-start = (bf16[192,4096]{1,0:T(8,128)(2,1)}, bf16[192,4096]{1,0:T(8,128)(2,1)S(1)}, u32[]{:S(2)}, u32[]{:S(2)}) collective-permute-start(bf16[192,4096]{1,0:T(8,128)(2,1)} %param.4), channel_id=1, source_target_pairs={{0,1},{1,2},{2,3},{3,0},{4,5},{5,6},{6,7},{7,4},{8,9},{9,10},{10,1... | collective-permute-start | bytes 4718600 | tf_op jit(solution)/shard_map/ppermute | solution.py:11
  47.6 37.5 %collective-permute-start.1 = (bf16[192,4096]{1,0:T(8,128)(2,1)S(1)}, bf16[192,4096]{1,0:T(8,128)(2,1)}, u32[]{:S(2)}, u32[]{:S(2)}) collective-permute-start(bf16[192,4096]{1,0:T(8,128)(2,1)S(1)} %collective-permute-done), channel_id=1, source_target_pairs={{0,1},{1,2},{2,3},{3,0},{4,5},{5,6},{6,7},{7,4},{8,9},{9,10},{10,1... | collective-permute-start | bytes 4718600 | tf_op jit(solution)/shard_map/ppermute | solution.py:11
  85.1 36.8 %collective-permute-start.2 = (bf16[192,4096]{1,0:T(8,128)(2,1)}, bf16[192,4096]{1,0:T(8,128)(2,1)}, u32[]{:S(2)}, u32[]{:S(2)}) collective-permute-start(bf16[192,4096]{1,0:T(8,128)(2,1)} %collective-permute-done.1), channel_id=1, source_target_pairs={{0,1},{1,2},{2,3},{3,0},{4,5},{5,6},{6,7},{7,4},{8,9},{9,10},{10,1... | collective-permute-start | bytes 4718600 | tf_op jit(solution)/shard_map/ppermute | solution.py:11
  142.4 8.1 %copy-start.1 = (bf16[4096]{0:T(1024)(128)(2,1)S(1)}, bf16[4096]{0:T(1024)(128)(2,1)}, u32[]{:S(2)}) copy-start(bf16[4096]{0:T(1024)(128)(2,1)} %param.6) | copy-start | bytes 24580
  142.5 17.0 %copy-start.3 = (s32[192]{0:T(256)S(1)}, s32[192]{0:T(256)}, u32[]{:S(2)}) copy-start(s32[192]{0:T(256)} %param.5) | copy-start | bytes 2308
  142.5 17.0 %copy-start.4 = (u32[32]{0:T(128)S(1)}, u32[32]{0:T(128)}, u32[]{:S(2)}) copy-start(u32[32]{0:T(128)} %constant.43) | copy-start | bytes 388
  142.5 108.7 %copy-start.2 = (f32[4096]{0:T(1024)S(1)}, f32[4096]{0:T(1024)}, u32[]{:S(2)}) copy-start(f32[4096]{0:T(1024)} %param.7) | copy-start | bytes 49156
  145.8 106.0 %all-to-all-start = ((bf16[192,8,2048]{2,0,1:T(8,128)(2,1)}), bf16[192,8,2048]{2,0,1:T(8,128)(2,1)}, u32[]{:S(2)}, u32[]{:S(2)}) async-start(bf16[192,8,2048]{2,0,1:T(8,128)(2,1)} %bitcast.15), calls=%async_computation | async-start | bytes 12582912 | tf_op jit(solution)/shard_map/all_to_all | solution.py:37
Sparse Core Ops, SparseCore 0:
  9.9 74.7 all-gather.1
